TPU v7x, 32 devices: a whole 2x2x4 slice. The times are simulated.
32 devices in a mesh: groups: 2 (over x), pts: 16 (over z, y, core).
Axes of the slice: x: 2, y: 2, z: 4, core: 2. Of those that a mesh axis runs over, the one named last changes fastest.
Arguments:
- points: float32 [32, 8192], P(None, ('groups', 'pts')), parts along dimension 1, may hold values from -6 to 6
- lengthscales: float32 [32], replicated, may hold values from 1.4 to 3
- noise: float32 [8192], P(('groups', 'pts')), parts along dimension 0, may hold values from 0.2 to 1
- targets: float32 [32, 8192], P(None, ('groups', 'pts')), parts along dimension 1, may hold values from -6 to 6
Outputs:
- solution: float32 [32, 8192], P(None, ('groups', 'pts')), parts along dimension 1
- residual: float32 [32, 8192], P(None, ('groups', 'pts')), parts along dimension 1
There are 2 independent parts, one for each index of `groups`. A program takes and returns all parts, laid end to end along the dimension named above; an argument that names none is the same for every part. Nothing has to cross between parts.
All inputs are finite; a program needn't handle non-finite values.
Results may differ from a plain program's by a relative error of at most 0.0045.
Values sent between devices are 32-bit elements; how exact they have to be, the bound alone decides.
A program may use at most 64 MiB of HBM per device.

v0:
```python
import math

import jax
import jax.numpy as jnp
from jax import lax
from jax.sharding import PartitionSpec as P

ITERS = 3


root_five = math.sqrt(5.0)


def matern(left, right):
    cross = jnp.dot(
        left.T, right, precision=lax.Precision.HIGHEST, preferred_element_type=jnp.float32
    )
    dist2 = (
        jnp.sum(left * left, axis=0)[:, None]
        + jnp.sum(right * right, axis=0)[None, :]
        - 2.0 * cross
    )
    scaled_dist = root_five * jnp.sqrt(jnp.maximum(dist2, 0.0))
    return (1.0 + scaled_dist + scaled_dist * scaled_dist / 3.0) * jnp.exp(-scaled_dist)


def gram(left, right):
    return lax.dot_general(
        left,
        right,
        (((1,), (1,)), ((), ())),
        precision=lax.Precision.HIGHEST,
        preferred_element_type=jnp.float32,
    )


def symmetric(matrix):
    return 0.5 * (matrix + matrix.T)


def spd_solve(matrix, right):
    lower = jnp.linalg.cholesky(matrix)
    return jax.scipy.linalg.cho_solve((lower, True), right)


def product(left, right):
    return jnp.dot(left, right, precision=lax.Precision.HIGHEST, preferred_element_type=jnp.float32)


def accumulate(total, feat_piece, dir_piece, own):
    width = feat_piece.shape[1]
    block_cols = 256

    def one_block(index, carry):
        begin = index * block_cols
        feats = lax.dynamic_slice_in_dim(feat_piece, begin, block_cols, 1)
        dirs = lax.dynamic_slice_in_dim(dir_piece, begin, block_cols, 1)
        return carry + product(dirs, matern(feats, own))

    return lax.fori_loop(0, width // block_cols, one_block, total)


def residual_norm(residual):
    return symmetric(lax.psum(gram(residual, residual), "pts"))


def body(points, lengthscales, noise, targets):
    scaled = points / lengthscales[:, None]
    solution = jnp.zeros_like(targets)
    residual = targets
    direction = targets
    norm_now = residual_norm(residual)
    for step in range(ITERS):
        empty = jnp.zeros(direction.shape, jnp.float32)
        image = accumulate(
            empty,
            lax.all_gather(scaled, "pts", axis=1, tiled=True),
            lax.all_gather(direction, "pts", axis=1, tiled=True),
            scaled,
        )
        image = image + noise[None, :] * direction
        curv = symmetric(lax.psum(gram(direction, image), "pts"))
        alpha = spd_solve(curv, norm_now)
        solution = solution + product(alpha.T, direction)
        residual = residual - product(alpha.T, image)
        if step + 1 < ITERS:
            norm_next = residual_norm(residual)
        if step + 1 < ITERS:
            beta = spd_solve(norm_now, norm_next)
            direction = residual + product(beta.T, direction)
            norm_now = norm_next
    return (solution, residual)


def solution(mesh):
    placed = (P(None, ("groups", "pts")), P(), P(("groups", "pts")), P(None, ("groups", "pts")))
    return jax.shard_map(
        body,
        mesh=mesh,
        in_specs=placed,
        out_specs=(P(None, ("groups", "pts")), P(None, ("groups", "pts"))),
        check_vma=False,
    )
```

profile of v0, /device:TPU:0, one launch (start us, length us, event | category | flops | bytes accessed | tf_op | source)
XLA Modules:
  0.0 458.8 jit_solution(8361852773679806300)
XLA Ops:
  0.6 1.0 fusion.105
  1.7 24.6 %all_gather.14 = f32[32,4096]{1,0:T(8,128)S(1)} all-gather(f32[32,256]{1,0:T(8,128)S(1)} %copy-done), channel_id=1, replica_groups=mesh['groups'=2,'pts'=16] {'pts'}, dimensions={1}, use_global_device_ids=true | all-gather | bytes 557056 | tf_op jit(solution)/shard_map/all_gather | solution.py:78
  26.4 18.9 %all_gather.15 = f32[32,4096]{1,0:T(8,128)S(1)} all-gather(f32[32,256]{1,0:T(8,128)S(1)} %get-tuple-element.687), channel_id=1, replica_groups=mesh['groups'=2,'pts'=16] {'pts'}, dimensions={1}, use_global_device_ids=true | all-gather | bytes 557056 | tf_op jit(solution)/shard_map/all_gather | solution.py:77
  45.3 13.7 %while.48 = (s32[]{:T(128)}, f32[32,256]{1,0:T(8,128)S(1)}, f32[32,4096]{1,0:T(8,128)S(1)}, f32[32,4096]{1,0:T(8,128)S(1)}, f32[256]{0:T(256)S(1)}, /*index=5*/f...) while((s32[]{:T(128)}, f32[32,256]{1,0:T(8,128)S(1)}, ...), condition=%wide.region_3.4_spmd.clone, body=%wide.region_1.3_spmd.clone.sunk | while | flops 51085060 | bytes 724145 | solution.py:60
  47.0 0.5 fusion.161
  48.7 0.5 fusion.161
  49.6 0.5 fusion.161
  58.9 0.7 copy-done.1
  59.8 59.2 %all-reduce = (f32[32,32]{1,0:T(8,128)S(1)}, f32[32,32]{1,0:T(8,128)S(1)}) all-reduce(f32[32,32]{1,0:T(8,128)S(1)} %fusion.105, f32[32,32]{1,0:T(8,128)S(1)} %convolution_bitcast_fusion), channel_id=1, replica_groups=mesh['groups'=2,'pts'=16] {'pts'}, use_global_device_ids=true, to_apply=%region_7.9 | all-reduce | flops 2048 | bytes 16384 | tf_op jit(solution)/shard_map/psum | solution.py:64
  119.2 2.9 cholesky.89
  122.1 0.6 compare_reduce_fusion.4
  122.8 0.7 fusion.59
  123.4 2.4 custom-call.14
  126.9 57.6 %psum.44 = f32[32,32]{1,0:T(8,128)S(1)} all-reduce(f32[32,32]{1,0:T(8,128)S(1)} %fusion.107), channel_id=1, replica_groups=mesh['groups'=2,'pts'=16] {'pts'}, use_global_device_ids=true, to_apply=%region_8.11 | all-reduce | flops 1024 | bytes 8192 | tf_op jit(solution)/shard_map/psum | solution.py:64
  184.7 2.9 cholesky.100
  187.6 0.6 compare_reduce_fusion.3
  188.3 0.7 fusion.60
  188.9 2.4 custom-call.15
  192.0 18.7 %all_gather.16 = f32[32,4096]{1,0:T(8,128)S(1)} all-gather(f32[32,256]{1,0:T(8,128)S(1)} %convolution_add_fusion.6), channel_id=1, replica_groups=mesh['groups'=2,'pts'=16] {'pts'}, dimensions={1}, use_global_device_ids=true | all-gather | bytes 557056 | tf_op jit(solution)/shard_map/all_gather | solution.py:78
  210.7 13.7 %while.49 = (s32[]{:T(128)}, f32[32,256]{1,0:T(8,128)S(1)}, f32[32,4096]{1,0:T(8,128)S(1)}, f32[32,4096]{1,0:T(8,128)S(1)}, f32[256]{0:T(256)S(1)}, /*index=5*/f...) while((s32[]{:T(128)}, f32[32,256]{1,0:T(8,128)S(1)}, ...), condition=%wide.region_11.0_spmd.clone, body=%wide.region_9.13_spmd.clone.sunk | while | flops 51085060 | bytes 724145 | solution.py:60
  211.6 0.5 fusion.166
  212.4 0.5 fusion.166
  213.3 0.5 fusion.166
  215.0 0.5 fusion.166
  215.9 0.5 fusion.166
  218.4 0.5 fusion.166
  219.3 0.5 fusion.166
  221.9 0.5 fusion.166
  222.7 0.5 fusion.166
  224.6 59.8 %psum.45 = f32[32,32]{1,0:T(8,128)S(1)} all-reduce(f32[32,32]{1,0:T(8,128)S(1)} %fusion.57), channel_id=1, replica_groups=mesh['groups'=2,'pts'=16] {'pts'}, use_global_device_ids=true, to_apply=%region_12.0 | all-reduce | flops 1024 | bytes 8192 | tf_op jit(solution)/shard_map/psum | solution.py:82
  284.6 2.9 cholesky.111
  287.5 0.6 compare_reduce_fusion.2
  288.2 0.7 fusion.61
  288.8 2.4 custom-call.16
  292.2 2.9 cholesky.122
  295.2 0.6 compare_reduce_fusion.1
  295.8 0.7 fusion.62
  296.5 2.4 custom-call.17
  299.1 57.7 %psum.46 = f32[32,32]{1,0:T(8,128)S(1)} all-reduce(f32[32,32]{1,0:T(8,128)S(1)} %fusion.108), channel_id=1, replica_groups=mesh['groups'=2,'pts'=16] {'pts'}, use_global_device_ids=true, to_apply=%region_13.16 | all-reduce | flops 1024 | bytes 8192 | tf_op jit(solution)/shard_map/psum | solution.py:64
  357.5 18.7 %all_gather.17 = f32[32,4096]{1,0:T(8,128)S(1)} all-gather(f32[32,256]{1,0:T(8,128)S(1)} %convolution_add_fusion.4), channel_id=1, replica_groups=mesh['groups'=2,'pts'=16] {'pts'}, dimensions={1}, use_global_device_ids=true | all-gather | bytes 557056 | tf_op jit(solution)/shard_map/all_gather | solution.py:78
  376.2 13.7 %while.50 = (s32[]{:T(128)}, f32[32,256]{1,0:T(8,128)S(1)}, f32[32,4096]{1,0:T(8,128)S(1)}, f32[32,4096]{1,0:T(8,128)S(1)}, f32[256]{0:T(256)S(1)}, /*index=5*/f...) while((s32[]{:T(128)}, f32[32,256]{1,0:T(8,128)S(1)}, ...), condition=%wide.region_16.0_spmd.clone, body=%wide.region_14.18_spmd.clone.sunk | while | flops 51085060 | bytes 724145 | solution.py:60
  390.0 59.9 %psum.47 = f32[32,32]{1,0:T(8,128)S(1)} all-reduce(f32[32,32]{1,0:T(8,128)S(1)} %fusion.58), channel_id=1, replica_groups=mesh['groups'=2,'pts'=16] {'pts'}, use_global_device_ids=true, to_apply=%region_17.0 | all-reduce | flops 1024 | bytes 8192 | tf_op jit(solution)/shard_map/psum | solution.py:82
  450.1 2.9 cholesky.133
  453.0 0.6 compare_reduce_fusion
  453.7 0.7 fusion.63
  454.3 2.4 custom-call.18
  457.1 0.9 convolution_add_fusion.3
  458.0 0.8 convolution_subtract_fusion
  (189 shorter events, 38.4 us)
Async XLA Ops:
  0.6 1.0 copy-start
  1.7 24.6 %copy-start.2 = (f32[32,256]{1,0:T(8,128)S(1)}, f32[32,256]{1,0:T(8,128)}, u32[]{:S(2)}) copy-start(f32[32,256]{1,0:T(8,128)} %param.13) | copy-start | bytes 98308
  1.7 24.6 %copy-start.3 = (f32[32]{0:T(128)S(1)}, f32[32]{0:T(128)}, u32[]{:S(2)}) copy-start(f32[32]{0:T(128)} %param.14) | copy-start | bytes 388
  58.9 0.7 copy-start.1
where the time goes:
time: 459 us
  blocking collectives  375 us (82%)
  matrix products  44.7 us (10%)
  other arithmetic  34.9 us (8%)
    psum x3, blocking collectives, residual_norm(): return symmetric(lax.psum(gram(residual, residual), 'pts'))  174 us
    psum x2, blocking collectives, body(): curv = symmetric(lax.psum(gram(direction, image), 'pts'))  120 us
    all_gather x3, blocking collectives, body(): lax.all_gather(direction, 'pts', axis=1, tiled=True)  62 us
    dot_general x48, matrix products, matern(): jnp.dot(left.T, right, precision=lax.Precision.HIGHEST, preferred_element...  23.6 us
    all_gather x1, blocking collectives, body(): lax.all_gather(scaled, 'pts', axis=1, tiled=True)  18.9 us
    another operation x15, other arithmetic, spd_solve(): lower = jnp.linalg.cholesky(matrix)  18 us
    dot_general x56, matrix products, product(): jnp.dot(left, right, precision=lax.Precision.HIGHEST, preferred_element_t...  17.4 us
    another operation x10, other arithmetic, spd_solve(): return jax.scipy.linalg.cho_solve((lower, True), right)  15.4 us

commit v1 on v0

v1 whole, which is shorter than its diff:
```python
import functools

import jax
import jax.numpy as jnp
from jax import lax
from jax.experimental import pallas as pl
from jax.experimental.pallas import tpu as pltpu
from jax.sharding import PartitionSpec as P

ITERS = 3
MESH = pl.DeviceIdType.MESH
NT = (((1,), (1,)), ((), ()))
NN = (((1,), (0,)), ((), ()))
F32 = jnp.float32
BF16 = jnp.bfloat16


def mxu(left, right, dims):
    return lax.dot_general(left, right, dims, preferred_element_type=F32)


def split3(x):
    hi = x.astype(BF16)
    rest = x - hi.astype(F32)
    mid = rest.astype(BF16)
    low = (rest - mid.astype(F32)).astype(BF16)
    return hi, mid, low


def stack3(x):
    return jnp.concatenate(split3(x), axis=0)


def six_rows(stacked, rows):
    return jnp.concatenate([stacked, stacked[: 2 * rows], stacked[:rows]], axis=0)


def six_lanes(x):
    hi, mid, low = split3(x)
    wide = [hi, hi, hi, mid, mid, low]
    return jnp.concatenate([w.astype(F32) for w in wide], axis=1).astype(BF16)


def fold_gram(g, rows):
    r = rows
    total = g[2 * r :, :r] + g[r : 2 * r, r : 2 * r] + g[:r, 2 * r :]
    total = total + (g[r : 2 * r, :r] + g[:r, r : 2 * r])
    total = total + g[:r, :r]
    return 0.5 * (total + total.T)


def eliminate(systems, size):
    rows = lax.broadcasted_iota(jnp.int32, systems[0].shape, 0)
    for j in range(size):
        done = []
        for m in systems:
            col = jnp.broadcast_to(m[:, j : j + 1], m.shape)
            row = m[j : j + 1, :] / col[j : j + 1, :]
            done.append(jnp.where(rows == j, row, m - col * row))
        systems = done
    return [m[:, size : 2 * size] for m in systems]


def augmented(matrix, right):
    rows, size = matrix.shape
    pad = jnp.zeros((rows, 128 - 2 * size), F32)
    return jnp.concatenate([matrix, right, pad], axis=1)


def matern_tile(own, own_norm, feats):
    cross = mxu(own, six_rows(stack3(feats), feats.shape[0]), NN)
    norm = jnp.sum(feats * feats, axis=0, keepdims=True)
    d2 = own_norm + norm - 2.0 * cross
    x = jnp.maximum(5.0 * d2, 1e-30)
    t = x * lax.rsqrt(x)
    return (1.0 + t + x * (1.0 / 3.0)) * jnp.exp(-t)


def kernel(
    n, pts_ref, ls_ref, noise_ref, tgt_ref, sol_ref, res_ref,
    gbuf, qbuf, pbuf, kth, ktl, dst, qst, rbuf, own_t, own_n, q_own, d_own,
    acc_h, acc_l, gram,
    send1, send2, recv, send_p, recv_p,
):
    me = lax.axis_index("pts")
    chips = n // 2
    chip = me // 2
    core = lax.rem(me, 2)
    sibling = 2 * chip + 1 - core
    f, width = pts_ref.shape
    r = tgt_ref.shape[0]

    barrier = pltpu.get_barrier_semaphore()

    def greet(s, c):
        peer = lax.rem(me + s, n)
        pl.semaphore_signal(barrier, inc=1, device_id={"pts": peer}, device_id_type=MESH)
        return c

    lax.fori_loop(1, n, greet, 0)

    scaled = pts_ref[...] / ls_ref[...]
    gbuf[me, :f, :] = scaled
    gbuf[me, f:, :] = tgt_ref[...]
    scaled_t = scaled.T
    own_t[...] = six_lanes(scaled_t)
    own_n[...] = jnp.broadcast_to(jnp.sum(scaled_t * scaled_t, axis=1, keepdims=True), own_n.shape)
    d_own[...] = tgt_ref[...]

    pl.semaphore_wait(barrier, n - 1)

    def to_plane(rnd, buf, s):
        to = 2 * lax.rem(chip + s, chips) + core
        return pltpu.make_async_remote_copy(
            src_ref=buf.at[me], dst_ref=buf.at[me],
            send_sem=send1.at[rnd, s], recv_sem=recv.at[rnd, me],
            device_id={"pts": to}, device_id_type=MESH,
        )

    def to_sibling(rnd, buf, s, slot):
        return pltpu.make_async_remote_copy(
            src_ref=buf.at[slot], dst_ref=buf.at[slot],
            send_sem=send2.at[rnd, s], recv_sem=recv.at[rnd, slot],
            device_id={"pts": sibling}, device_id_type=MESH,
        )

    def source(s):
        return 2 * lax.rem(chip + chips - s, chips)

    def gather_start(rnd, buf):
        to_sibling(rnd, buf, 0, me).start()

        def one(s, c):
            to_plane(rnd, buf, s).start()
            return c

        lax.fori_loop(1, chips, one, 0)

    def gather_use(rnd, buf, use):
        use(me)
        to_sibling(rnd, buf, 0, sibling).wait_recv()
        use(sibling)

        def plane(s, c):
            slot = source(s) + core
            copy = to_sibling(rnd, buf, s, slot)
            copy.wait_recv()
            copy.start()
            use(slot)
            return c

        def other(s, c):
            slot = source(s) + 1 - core
            to_sibling(rnd, buf, s, slot).wait_recv()
            use(slot)
            return c

        lax.fori_loop(1, chips, plane, 0)
        lax.fori_loop(1, chips, other, 0)

    gather_start(0, gbuf)
    acc_h[...] = jnp.zeros_like(acc_h)
    acc_l[...] = jnp.zeros_like(acc_l)
    gram[...] = jnp.zeros_like(gram)

    def first(slot):
        tile = matern_tile(own_t[...], own_n[...], gbuf[slot, :f, :])
        high = tile.astype(BF16)
        low = (tile - high.astype(F32)).astype(BF16)
        kth[slot] = high
        ktl[slot] = low
        values = gbuf[slot, f:, :]
        rbuf[slot] = values
        stacked = stack3(values)
        dst[slot] = stacked
        gram[...] += mxu(stacked, stacked, NT)
        acc_h[...] += mxu(stacked, high, NT)
        acc_l[...] += mxu(stacked[: 2 * r], low, NT)

    gather_use(0, gbuf, first)
    rr = fold_gram(gram[...], r)
    eye = (
        lax.broadcasted_iota(jnp.int32, (r, r), 0) == lax.broadcasted_iota(jnp.int32, (r, r), 1)
    ).astype(F32)

    def image_own():
        h = acc_h[...]
        l = acc_l[...]
        return (h[2 * r :] + l[r:]) + (h[r : 2 * r] + l[:r]) + h[:r] + noise_ref[...] * d_own[...]

    solution = jnp.zeros((r, width), F32)
    for step in range(ITERS - 1):
        buf = qbuf.at[step]
        buf[me] = image_own()
        gather_start(step + 1, buf)
        gram[...] = jnp.zeros_like(gram)

        def curvature(slot, buf=buf):
            stacked = stack3(buf[slot])
            qst[slot] = stacked
            gram[...] += mxu(dst[slot], stacked, NT)

        gather_use(step + 1, buf, curvature)
        alpha, rr_inv = eliminate(
            [augmented(fold_gram(gram[...], r), rr), augmented(rr, eye)], r
        )
        alpha_t = six_lanes(alpha.T)
        solution = solution + mxu(alpha_t, six_rows(dst[me], r), NN)
        gram[...] = jnp.zeros_like(gram)

        def residuals(s, c, alpha_t=alpha_t):
            value = rbuf[s] - mxu(alpha_t, six_rows(qst[s], r), NN)
            rbuf[s] = value
            stacked = stack3(value)
            gram[...] += mxu(stacked, stacked, NT)
            return c

        lax.fori_loop(0, n, residuals, 0)
        rr_next = fold_gram(gram[...], r)
        beta = jnp.dot(rr_inv, rr_next, precision=lax.Precision.HIGHEST, preferred_element_type=F32)
        beta_t = six_lanes(beta.T)
        d_own[...] = rbuf[me] + mxu(beta_t, six_rows(dst[me], r), NN)
        acc_h[...] = jnp.zeros_like(acc_h)
        acc_l[...] = jnp.zeros_like(acc_l)

        def directions(s, c, beta_t=beta_t):
            value = rbuf[s] + mxu(beta_t, six_rows(dst[s], r), NN)
            stacked = stack3(value)
            dst[s] = stacked
            acc_h[...] += mxu(stacked, kth[s], NT)
            acc_l[...] += mxu(stacked[: 2 * r], ktl[s], NT)
            return c

        lax.fori_loop(0, n, directions, 0)
        rr = rr_next

    q_own[...] = image_own()
    q_stacked = stack3(q_own[...])
    g = mxu(dst[me], q_stacked, NT)
    partial = fold_gram(g, r)
    pbuf[me] = jnp.concatenate([partial, jnp.zeros((r, 128 - r), F32)], axis=1)

    def to_peer(s, slot):
        return pltpu.make_async_remote_copy(
            src_ref=pbuf.at[slot], dst_ref=pbuf.at[slot],
            send_sem=send_p.at[s], recv_sem=recv_p.at[slot],
            device_id={"pts": lax.rem(me + s, n)}, device_id_type=MESH,
        )

    def give(s, c):
        to_peer(s, me).start()
        return c

    lax.fori_loop(1, n, give, 0)

    def take(s, c):
        to_peer(s, lax.rem(me + n - s, n)).wait_recv()
        return c

    lax.fori_loop(1, n, take, 0)
    total = lax.fori_loop(0, n, lambda s, c: c + pbuf[s], jnp.zeros((r, 128), F32))
    (alpha,) = eliminate([augmented(total[:, :r], rr)], r)
    alpha_t = six_lanes(alpha.T)
    sol_ref[...] = solution + mxu(alpha_t, six_rows(dst[me], r), NN)
    res_ref[...] = rbuf[me] - mxu(alpha_t, six_rows(q_stacked, r), NN)

    def drain(s, c):
        for rnd in range(ITERS):
            buf = gbuf if rnd == 0 else qbuf.at[rnd - 1]
            to_plane(rnd, buf, s).wait_send()
            to_sibling(rnd, buf, s, me).wait_send()
        return c

    for rnd in range(ITERS):
        buf = gbuf if rnd == 0 else qbuf.at[rnd - 1]
        to_sibling(rnd, buf, 0, me).wait_send()
    lax.fori_loop(1, chips, drain, 0)

    def drain_peer(s, c):
        to_peer(s, me).wait_send()
        return c

    lax.fori_loop(1, n, drain_peer, 0)


def body(n, points, lengthscales, noise, targets):
    f, width = points.shape
    r = targets.shape[0]
    block = jax.ShapeDtypeStruct((r, width), F32)
    vmem = pl.BlockSpec(memory_space=pltpu.VMEM)
    return pl.pallas_call(
        functools.partial(kernel, n),
        out_shape=(block, block),
        in_specs=[vmem] * 4,
        out_specs=(vmem, vmem),
        scratch_shapes=[
            pltpu.VMEM((n, f + r, width), F32),
            pltpu.VMEM((ITERS - 1, n, r, width), F32),
            pltpu.VMEM((n, r, 128), F32),
            pltpu.VMEM((n, width, width), BF16),
            pltpu.VMEM((n, width, width), BF16),
            pltpu.VMEM((n, 3 * r, width), BF16),
            pltpu.VMEM((n, 3 * r, width), BF16),
            pltpu.VMEM((n, r, width), F32),
            pltpu.VMEM((width, 6 * f), BF16),
            pltpu.VMEM((width, width), F32),
            pltpu.VMEM((r, width), F32),
            pltpu.VMEM((r, width), F32),
            pltpu.VMEM((3 * r, width), F32),
            pltpu.VMEM((2 * r, width), F32),
            pltpu.VMEM((3 * r, 3 * r), F32),
            pltpu.SemaphoreType.DMA((ITERS, n // 2)),
            pltpu.SemaphoreType.DMA((ITERS, n // 2)),
            pltpu.SemaphoreType.DMA((ITERS, n)),
            pltpu.SemaphoreType.DMA((n,)),
            pltpu.SemaphoreType.DMA((n,)),
        ],
        compiler_params=pltpu.CompilerParams(
            collective_id=0, has_side_effects=True, vmem_limit_bytes=56 * 1024 * 1024
        ),
    )(points, lengthscales[:, None], noise[None, :], targets)


def solution(mesh):
    wide = P(None, ("groups", "pts"))
    return jax.shard_map(
        functools.partial(body, mesh.shape["pts"]),
        mesh=mesh,
        in_specs=(wide, P(), P(("groups", "pts")), wide),
        out_specs=(wide, wide),
        check_vma=False,
    )
```

time: 459 us -> 84 us (0.18)
  blocking collectives: 375 us -> 0 us
  Pallas kernels: 0 us -> 79.4 us
  matrix products: 44.7 us -> 0 us
  other arithmetic: 34.9 us -> 0 us
    psum x5 -> x0, blocking collectives: 294 us -> none  [the longest x3 174 us: residual_norm(): return symmetric(lax.psum(gram(residual, residual), 'pts'))]
    all_gather x4 -> x0, blocking collectives: 80.9 us -> none  [the longest x3 62 us: body(): lax.all_gather(direction, 'pts', axis=1, tiled=True)]
    pallas_call x0 -> x1, Pallas kernels: none -> 79.4 us  [body(): pl.pallas_call(functools.partial(kernel, n), out_shape=(block, block), in...]
    dot_general x110 -> x0, matrix products: 42.8 us -> none  [the longest x48 23.6 us: matern(): jnp.dot(left.T, right, precision=lax.Precision.HIGHEST, preferred_element...]
    another operation x25 -> x0, other arithmetic: 33.4 us -> none  [the longest x15 18 us: spd_solve(): lower = jnp.linalg.cholesky(matrix)]
where the time goes in v1:
time: 84 us; the launch traced here: 83.3 us
  Pallas kernels  79.4 us (95%)
  local copies, waits for them, and re-layouts  3.34 us (4%)
    pallas_call x1, Pallas kernels, body(): pl.pallas_call(functools.partial(kernel, n), out_shape=(block, block), in...  79.4 us
    unnamed x6, local copies, waits for them, and re-layouts  2.65 us

profile of v1, /device:TPU:0, one launch (start us, length us, event | category | flops | bytes accessed | tf_op | source)
XLA Modules:
  0.0 83.3 jit_solution(3294988056343634334)
XLA Ops:
  0.6 0.0 copy-start.1
  0.6 0.6 copy-done.1
  1.3 0.7 copy.6.ls_ref
  2.0 79.4 %shard_map.59 = (f32[32,256]{1,0:T(8,128)}, f32[32,256]{1,0:T(8,128)}) custom-call(f32[32,256]{1,0:T(8,128)} %pts_ref.1, f32[32,1]{1,0:T(8,128)} %copy.6.ls_ref, f32[1,256]{1,0:T(1,128)} %bitcast.2, f32[32,256]{1,0:T(8,128)} %tgt_ref.1), custom_call_target="tpu_custom_call" | custom-call | tf_op jit(solution)/shard_map/pallas_call | solution.py:291
  81.3 0.0 copy-start
  81.3 1.4 %copy.9 = f32[32,256]{1,0:T(8,128)} copy(f32[32,256]{1,0:T(8,128)} %get-tuple-element.4) | data formatting | bytes 65536
  82.7 0.0 copy-done
  82.7 0.6 copy.10
Async XLA Ops:
  0.6 0.7 copy-start.1
  81.3 1.4 %copy-start = (f32[32,256]{1,0:T(8,128)S(1)}, f32[32,256]{1,0:T(8,128)}, u32[]{:S(2)}) copy-start(f32[32,256]{1,0:T(8,128)} %get-tuple-element.5) | copy-start | bytes 98308

commit v2 on v1

--- a/solution.py
+++ b/solution.py
@@ -51,12 +51,21 @@
 
 def eliminate(systems, size):
     rows = lax.broadcasted_iota(jnp.int32, systems[0].shape, 0)
-    for j in range(size):
+    for j in range(0, size, 2):
+        i = j + 1
         done = []
         for m in systems:
-            col = jnp.broadcast_to(m[:, j : j + 1], m.shape)
-            row = m[j : j + 1, :] / col[j : j + 1, :]
-            done.append(jnp.where(rows == j, row, m - col * row))
+            left = jnp.broadcast_to(m[:, j : j + 1], m.shape)
+            right = jnp.broadcast_to(m[:, i : i + 1], m.shape)
+            first, second = m[j : j + 1, :], m[i : i + 1, :]
+            inv = 1.0 / left[j : j + 1, :]
+            ratio = right[j : j + 1, :] * inv
+            below = left[i : i + 1, :]
+            schur = right[i : i + 1, :] - below * ratio
+            second = (second - below * (first * inv)) / schur
+            first = first * inv - ratio * second
+            m = m - (left * first + right * second)
+            done.append(jnp.where(rows == j, first, jnp.where(rows == i, second, m)))
         systems = done
     return [m[:, size : 2 * size] for m in systems]
 
@@ -77,16 +86,21 @@
 
 
 def kernel(
-    n, pts_ref, ls_ref, noise_ref, tgt_ref, sol_ref, res_ref,
+    n, wide, pts_ref, ls_ref, noise_ref, tgt_ref, sol_ref, res_ref,
     gbuf, qbuf, pbuf, kth, ktl, dst, qst, rbuf, own_t, own_n, q_own, d_own,
     acc_h, acc_l, gram,
-    send1, send2, recv, send_p, recv_p,
+    send_z, send_y, send_k, recv, send_p, recv_p,
 ):
     me = lax.axis_index("pts")
     chips = n // 2
+    deep = chips // wide
     chip = me // 2
     core = lax.rem(me, 2)
     sibling = 2 * chip + 1 - core
+    z, y = chip // wide, lax.rem(chip, wide)
+
+    def device(dz, dy):
+        return 2 * (lax.rem(z + dz, deep) * wide + lax.rem(y + dy, wide)) + core
     f, width = pts_ref.shape
     r = tgt_ref.shape[0]
 
@@ -109,75 +123,95 @@
 
     pl.semaphore_wait(barrier, n - 1)
 
-    def to_plane(rnd, buf, s):
-        to = 2 * lax.rem(chip + s, chips) + core
-        return pltpu.make_async_remote_copy(
-            src_ref=buf.at[me], dst_ref=buf.at[me],
-            send_sem=send1.at[rnd, s], recv_sem=recv.at[rnd, me],
-            device_id={"pts": to}, device_id_type=MESH,
-        )
-
-    def to_sibling(rnd, buf, s, slot):
+    def to(rnd, buf, slot, peer, send):
         return pltpu.make_async_remote_copy(
             src_ref=buf.at[slot], dst_ref=buf.at[slot],
-            send_sem=send2.at[rnd, s], recv_sem=recv.at[rnd, slot],
-            device_id={"pts": sibling}, device_id_type=MESH,
+            send_sem=send, recv_sem=recv.at[rnd, slot],
+            device_id={"pts": peer}, device_id_type=MESH,
         )
 
-    def source(s):
-        return 2 * lax.rem(chip + chips - s, chips)
+    def along_z(rnd, buf, dz):
+        return to(rnd, buf, me, device(dz, 0), send_z.at[rnd, dz])
+
+    def along_y(rnd, buf, dz, dy):
+        return to(rnd, buf, device(deep - dz, 0), device(0, dy), send_y.at[rnd, dz, dy])
+
+    def across(rnd, buf, dz, dy):
+        slot = device(deep - dz, wide - dy)
+        return to(rnd, buf, slot, sibling, send_k.at[rnd, dz, dy])
+
+    def loop(begin, end, one):
+        def run(s, c):
+            one(s)
+            return c
+
+        lax.fori_loop(begin, end, run, 0)
 
     def gather_start(rnd, buf):
-        to_sibling(rnd, buf, 0, me).start()
-
-        def one(s, c):
-            to_plane(rnd, buf, s).start()
-            return c
-
-        lax.fori_loop(1, chips, one, 0)
-
-    def gather_use(rnd, buf, use):
-        use(me)
-        to_sibling(rnd, buf, 0, sibling).wait_recv()
-        use(sibling)
-
-        def plane(s, c):
-            slot = source(s) + core
-            copy = to_sibling(rnd, buf, s, slot)
+        loop(1, deep, lambda dz: along_z(rnd, buf, dz).start())
+        for dy in range(1, wide):
+            along_y(rnd, buf, 0, dy).start()
+        across(rnd, buf, 0, 0).start()
+
+    def gather_use(rnd, buf, use, batch):
+        use([me])
+
+        def lane(dz):
+            copy = across(rnd, buf, dz, 0)
             copy.wait_recv()
+            for dy in range(1, wide):
+                along_y(rnd, buf, dz, dy).start()
             copy.start()
-            use(slot)
-            return c
-
-        def other(s, c):
-            slot = source(s) + 1 - core
-            to_sibling(rnd, buf, s, slot).wait_recv()
-            use(slot)
-            return c
-
-        lax.fori_loop(1, chips, plane, 0)
-        lax.fori_loop(1, chips, other, 0)
+            use([device(deep - dz, 0)])
+
+        loop(1, deep, lane)
+        for dy in range(1, wide):
+
+            def plane(dz, dy=dy):
+                copy = across(rnd, buf, dz, dy)
+                copy.wait_recv()
+                copy.start()
+                use([device(deep - dz, wide - dy)])
+
+            loop(0, deep, plane)
+
+        def other(s):
+            slots = []
+            for i in range(batch):
+                at = s * batch + i
+                slot = 2 * (lax.rem(z + deep - at // wide, deep) * wide + lax.rem(y + lax.rem(at, wide), wide)) + 1 - core
+                to(rnd, buf, slot, sibling, send_k.at[rnd, 0, 0]).wait_recv()
+                slots.append(slot)
+            use(slots)
+
+        loop(0, chips // batch, other)
+
+    def lanes(parts):
+        return parts[0] if len(parts) == 1 else jnp.concatenate(parts, axis=1)
 
     gather_start(0, gbuf)
     acc_h[...] = jnp.zeros_like(acc_h)
     acc_l[...] = jnp.zeros_like(acc_l)
     gram[...] = jnp.zeros_like(gram)
 
-    def first(slot):
-        tile = matern_tile(own_t[...], own_n[...], gbuf[slot, :f, :])
-        high = tile.astype(BF16)
-        low = (tile - high.astype(F32)).astype(BF16)
-        kth[slot] = high
-        ktl[slot] = low
-        values = gbuf[slot, f:, :]
-        rbuf[slot] = values
-        stacked = stack3(values)
-        dst[slot] = stacked
+    def first(slots):
+        stacks, highs, lows, values = [], [], [], [gbuf[slot, f:, :] for slot in slots]
+        for slot, value in zip(slots, values):
+            tile = matern_tile(own_t[...], own_n[...], gbuf[slot, :f, :])
+            highs.append(tile.astype(BF16))
+            lows.append((tile - highs[-1].astype(F32)).astype(BF16))
+            stacks.append(stack3(value))
+        stacked = lanes(stacks)
         gram[...] += mxu(stacked, stacked, NT)
-        acc_h[...] += mxu(stacked, high, NT)
-        acc_l[...] += mxu(stacked[: 2 * r], low, NT)
-
-    gather_use(0, gbuf, first)
+        acc_h[...] += mxu(stacked, lanes(highs), NT)
+        acc_l[...] += mxu(stacked[: 2 * r], lanes(lows), NT)
+        for slot, value, high, low, stack in zip(slots, values, highs, lows, stacks):
+            kth[slot] = high
+            ktl[slot] = low
+            rbuf[slot] = value
+            dst[slot] = stack
+
+    gather_use(0, gbuf, first, 2)
     rr = fold_gram(gram[...], r)
     eye = (
         lax.broadcasted_iota(jnp.int32, (r, r), 0) == lax.broadcasted_iota(jnp.int32, (r, r), 1)
@@ -195,12 +229,13 @@
         gather_start(step + 1, buf)
         gram[...] = jnp.zeros_like(gram)
 
-        def curvature(slot, buf=buf):
-            stacked = stack3(buf[slot])
-            qst[slot] = stacked
-            gram[...] += mxu(dst[slot], stacked, NT)
-
-        gather_use(step + 1, buf, curvature)
+        def curvature(slots, buf=buf):
+            stacks = [stack3(buf[slot]) for slot in slots]
+            gram[...] += mxu(lanes([dst[slot] for slot in slots]), lanes(stacks), NT)
+            for slot, stack in zip(slots, stacks):
+                qst[slot] = stack
+
+        gather_use(step + 1, buf, curvature, 4)
         alpha, rr_inv = eliminate(
             [augmented(fold_gram(gram[...], r), rr), augmented(rr, eye)], r
         )
@@ -208,14 +243,17 @@
         solution = solution + mxu(alpha_t, six_rows(dst[me], r), NN)
         gram[...] = jnp.zeros_like(gram)
 
-        def residuals(s, c, alpha_t=alpha_t):
-            value = rbuf[s] - mxu(alpha_t, six_rows(qst[s], r), NN)
-            rbuf[s] = value
+        def residuals(s, alpha_t=alpha_t):
+            slots = [s * 4 + i for i in range(4)]
+            value = lanes([rbuf[slot] for slot in slots]) - mxu(
+                alpha_t, six_rows(lanes([qst[slot] for slot in slots]), r), NN
+            )
             stacked = stack3(value)
             gram[...] += mxu(stacked, stacked, NT)
-            return c
-
-        lax.fori_loop(0, n, residuals, 0)
+            for i, slot in enumerate(slots):
+                rbuf[slot] = value[:, i * width : (i + 1) * width]
+
+        loop(0, n // 4, residuals)
         rr_next = fold_gram(gram[...], r)
         beta = jnp.dot(rr_inv, rr_next, precision=lax.Precision.HIGHEST, preferred_element_type=F32)
         beta_t = six_lanes(beta.T)
@@ -223,15 +261,18 @@
         acc_h[...] = jnp.zeros_like(acc_h)
         acc_l[...] = jnp.zeros_like(acc_l)
 
-        def directions(s, c, beta_t=beta_t):
-            value = rbuf[s] + mxu(beta_t, six_rows(dst[s], r), NN)
+        def directions(s, beta_t=beta_t):
+            slots = [s * 4 + i for i in range(4)]
+            value = lanes([rbuf[slot] for slot in slots]) + mxu(
+                beta_t, six_rows(lanes([dst[slot] for slot in slots]), r), NN
+            )
             stacked = stack3(value)
-            dst[s] = stacked
-            acc_h[...] += mxu(stacked, kth[s], NT)
-            acc_l[...] += mxu(stacked[: 2 * r], ktl[s], NT)
-            return c
-
-        lax.fori_loop(0, n, directions, 0)
+            acc_h[...] += mxu(stacked, lanes([kth[slot] for slot in slots]), NT)
+            acc_l[...] += mxu(stacked[: 2 * r], lanes([ktl[slot] for slot in slots]), NT)
+            for i, slot in enumerate(slots):
+                dst[slot] = stacked[:, i * width : (i + 1) * width]
+
+        loop(0, n // 4, directions)
         rr = rr_next
 
     q_own[...] = image_own()
@@ -264,17 +305,17 @@
     sol_ref[...] = solution + mxu(alpha_t, six_rows(dst[me], r), NN)
     res_ref[...] = rbuf[me] - mxu(alpha_t, six_rows(q_stacked, r), NN)
 
-    def drain(s, c):
-        for rnd in range(ITERS):
-            buf = gbuf if rnd == 0 else qbuf.at[rnd - 1]
-            to_plane(rnd, buf, s).wait_send()
-            to_sibling(rnd, buf, s, me).wait_send()
-        return c
-
     for rnd in range(ITERS):
         buf = gbuf if rnd == 0 else qbuf.at[rnd - 1]
-        to_sibling(rnd, buf, 0, me).wait_send()
-    lax.fori_loop(1, chips, drain, 0)
+
+        def drain(dz, rnd=rnd, buf=buf):
+            for dy in range(wide):
+                if dy > 0:
+                    along_y(rnd, buf, dz, dy).wait_send()
+                across(rnd, buf, dz, dy).wait_send()
+
+        loop(0, deep, drain)
+        loop(1, deep, lambda dz, rnd=rnd, buf=buf: along_z(rnd, buf, dz).wait_send())
 
     def drain_peer(s, c):
         to_peer(s, me).wait_send()
@@ -287,9 +328,12 @@
     f, width = points.shape
     r = targets.shape[0]
     block = jax.ShapeDtypeStruct((r, width), F32)
+    chips = n // 2
+    wide = 2 if chips % 2 == 0 and chips <= 8 else 1
+    deep = chips // wide
     vmem = pl.BlockSpec(memory_space=pltpu.VMEM)
     return pl.pallas_call(
-        functools.partial(kernel, n),
+        functools.partial(kernel, n, wide),
         out_shape=(block, block),
         in_specs=[vmem] * 4,
         out_specs=(vmem, vmem),
@@ -309,8 +353,9 @@
             pltpu.VMEM((3 * r, width), F32),
             pltpu.VMEM((2 * r, width), F32),
             pltpu.VMEM((3 * r, 3 * r), F32),
-            pltpu.SemaphoreType.DMA((ITERS, n // 2)),
-            pltpu.SemaphoreType.DMA((ITERS, n // 2)),
+            pltpu.SemaphoreType.DMA((ITERS, deep)),
+            pltpu.SemaphoreType.DMA((ITERS, deep, wide)),
+            pltpu.SemaphoreType.DMA((ITERS, deep, wide)),
             pltpu.SemaphoreType.DMA((ITERS, n)),
             pltpu.SemaphoreType.DMA((n,)),
             pltpu.SemaphoreType.DMA((n,)),

time: 84 us -> 65.7 us (0.78)
  Pallas kernels: 79.4 us -> 60.6 us
    pallas_call x1, Pallas kernels: 79.4 us -> 60.6 us  [body(): pl.pallas_call(functools.partial(kernel, n, wide), out_shape=(block, bloc...]
where the time goes in v2:
time: 65.7 us; the launch traced here: 64.6 us
  Pallas kernels  60.6 us (92%)
  local copies, waits for them, and re-layouts  3.34 us (5%)
  between operations  0.66 us (1%)
    pallas_call x1, Pallas kernels, body(): pl.pallas_call(functools.partial(kernel, n, wide), out_shape=(block, bloc...  60.6 us
    unnamed x6, local copies, waits for them, and re-layouts  2.65 us

profile of v2, /device:TPU:0, one launch (start us, length us, event | category | flops | bytes accessed | tf_op | source)
XLA Modules:
  0.0 64.6 jit_solution(6380700083907090273)
XLA Ops:
  0.6 0.0 copy-start.1
  0.6 0.6 copy-done.1
  1.3 0.7 %copy.6.ls_ref = f32[32,1]{1,0:T(8,128)} copy(f32[32,1]{0,1:T(1,128)S(1)} %bitcast.3) | data formatting | bytes 256 | tf_op jit(solution)/shard_map/broadcast_in_dim | solution.py:366
  2.0 60.6 %shard_map.59 = (f32[32,256]{1,0:T(8,128)}, f32[32,256]{1,0:T(8,128)}) custom-call(f32[32,256]{1,0:T(8,128)} %pts_ref.1, f32[32,1]{1,0:T(8,128)} %copy.6.ls_ref, f32[1,256]{1,0:T(1,128)} %bitcast.2, f32[32,256]{1,0:T(8,128)} %tgt_ref.1), custom_call_target="tpu_custom_call" | custom-call | tf_op jit(solution)/shard_map/pallas_call | solution.py:335
  62.6 0.0 copy-start
  62.6 1.4 %copy.9 = f32[32,256]{1,0:T(8,128)} copy(f32[32,256]{1,0:T(8,128)} %get-tuple-element.4) | data formatting | bytes 65536
  64.0 0.0 copy-done
  64.0 0.6 copy.10
Async XLA Ops:
  0.6 0.7 %copy-start.1 = (f32[32]{0:T(128)S(1)}, f32[32]{0:T(128)}, u32[]{:S(2)}) copy-start(f32[32]{0:T(128)} %param.5) | copy-start | bytes 388
  62.6 1.4 %copy-start = (f32[32,256]{1,0:T(8,128)S(1)}, f32[32,256]{1,0:T(8,128)}, u32[]{:S(2)}) copy-start(f32[32,256]{1,0:T(8,128)} %get-tuple-element.5) | copy-start | bytes 98308

commit v3 on v2

--- a/solution.py
+++ b/solution.py
@@ -87,7 +87,7 @@
 
 def kernel(
     n, wide, pts_ref, ls_ref, noise_ref, tgt_ref, sol_ref, res_ref,
-    gbuf, qbuf, pbuf, kth, ktl, dst, qst, rbuf, own_t, own_n, q_own, d_own,
+    gbuf, qbuf, pbuf, kth, ktl, dst, qst, rbuf, own_t, own_n, q_own,
     acc_h, acc_l, gram,
     send_z, send_y, send_k, recv, send_p, recv_p,
 ):
@@ -113,13 +113,12 @@
 
     lax.fori_loop(1, n, greet, 0)
 
-    scaled = pts_ref[...] / ls_ref[...]
+    scaled = pts_ref[...] / jnp.broadcast_to(ls_ref[...], (f, f)).T[:, :1]
     gbuf[me, :f, :] = scaled
     gbuf[me, f:, :] = tgt_ref[...]
     scaled_t = scaled.T
     own_t[...] = six_lanes(scaled_t)
     own_n[...] = jnp.broadcast_to(jnp.sum(scaled_t * scaled_t, axis=1, keepdims=True), own_n.shape)
-    d_own[...] = tgt_ref[...]
 
     pl.semaphore_wait(barrier, n - 1)
 
@@ -217,21 +216,40 @@
         lax.broadcasted_iota(jnp.int32, (r, r), 0) == lax.broadcasted_iota(jnp.int32, (r, r), 1)
     ).astype(F32)
 
-    def image_own():
+    def operator(own):
         h = acc_h[...]
         l = acc_l[...]
-        return (h[2 * r :] + l[r:]) + (h[r : 2 * r] + l[:r]) + h[:r] + noise_ref[...] * d_own[...]
+        return (h[2 * r :] + l[r:]) + (h[r : 2 * r] + l[:r]) + h[:r] + noise_ref[...] * own
 
     solution = jnp.zeros((r, width), F32)
+    image_r = operator(tgt_ref[...])
+    q_own[...] = image_r
     for step in range(ITERS - 1):
         buf = qbuf.at[step]
-        buf[me] = image_own()
+        buf[me] = q_own[...]
         gather_start(step + 1, buf)
+        if step > 0:
+
+            def directions(s, beta_t=beta_t):
+                slots = [s * 4 + i for i in range(4)]
+                value = lanes([rbuf[slot] for slot in slots]) + mxu(
+                    beta_t, six_rows(lanes([dst[slot] for slot in slots]), r), NN
+                )
+                stacked = stack3(value)
+                for i, slot in enumerate(slots):
+                    dst[slot] = stacked[:, i * width : (i + 1) * width]
+
+            loop(0, n // 4, directions)
         gram[...] = jnp.zeros_like(gram)
+        acc_h[...] = jnp.zeros_like(acc_h)
+        acc_l[...] = jnp.zeros_like(acc_l)
 
         def curvature(slots, buf=buf):
             stacks = [stack3(buf[slot]) for slot in slots]
-            gram[...] += mxu(lanes([dst[slot] for slot in slots]), lanes(stacks), NT)
+            stacked = lanes(stacks)
+            gram[...] += mxu(lanes([dst[slot] for slot in slots]), stacked, NT)
+            acc_h[...] += mxu(stacked, lanes([kth[slot] for slot in slots]), NT)
+            acc_l[...] += mxu(stacked[: 2 * r], lanes([ktl[slot] for slot in slots]), NT)
             for slot, stack in zip(slots, stacks):
                 qst[slot] = stack
 
@@ -241,6 +259,8 @@
         )
         alpha_t = six_lanes(alpha.T)
         solution = solution + mxu(alpha_t, six_rows(dst[me], r), NN)
+        image_q = operator(q_own[...])
+        image_r = image_r - mxu(alpha_t, six_rows(stack3(image_q), r), NN)
         gram[...] = jnp.zeros_like(gram)
 
         def residuals(s, alpha_t=alpha_t):
@@ -257,29 +277,15 @@
         rr_next = fold_gram(gram[...], r)
         beta = jnp.dot(rr_inv, rr_next, precision=lax.Precision.HIGHEST, preferred_element_type=F32)
         beta_t = six_lanes(beta.T)
-        d_own[...] = rbuf[me] + mxu(beta_t, six_rows(dst[me], r), NN)
-        acc_h[...] = jnp.zeros_like(acc_h)
-        acc_l[...] = jnp.zeros_like(acc_l)
-
-        def directions(s, beta_t=beta_t):
-            slots = [s * 4 + i for i in range(4)]
-            value = lanes([rbuf[slot] for slot in slots]) + mxu(
-                beta_t, six_rows(lanes([dst[slot] for slot in slots]), r), NN
-            )
-            stacked = stack3(value)
-            acc_h[...] += mxu(stacked, lanes([kth[slot] for slot in slots]), NT)
-            acc_l[...] += mxu(stacked[: 2 * r], lanes([ktl[slot] for slot in slots]), NT)
-            for i, slot in enumerate(slots):
-                dst[slot] = stacked[:, i * width : (i + 1) * width]
-
-        loop(0, n // 4, directions)
+        q_own[...] = image_r + mxu(beta_t, six_rows(qst[me], r), NN)
         rr = rr_next
 
-    q_own[...] = image_own()
+    dst[me] = stack3(rbuf[me] + mxu(beta_t, six_rows(dst[me], r), NN))
     q_stacked = stack3(q_own[...])
     g = mxu(dst[me], q_stacked, NT)
     partial = fold_gram(g, r)
-    pbuf[me] = jnp.concatenate([partial, jnp.zeros((r, 128 - r), F32)], axis=1)
+    piece = pbuf.shape[1]
+    pbuf[me] = jnp.concatenate([partial[i : i + piece] for i in range(0, r, piece)], axis=1)
 
     def to_peer(s, slot):
         return pltpu.make_async_remote_copy(
@@ -299,8 +305,9 @@
         return c
 
     lax.fori_loop(1, n, take, 0)
-    total = lax.fori_loop(0, n, lambda s, c: c + pbuf[s], jnp.zeros((r, 128), F32))
-    (alpha,) = eliminate([augmented(total[:, :r], rr)], r)
+    total = lax.fori_loop(0, n, lambda s, c: c + pbuf[s], jnp.zeros((piece, 128), F32))
+    total = jnp.concatenate([total[:, i : i + r] for i in range(0, 128, r)], axis=0)
+    (alpha,) = eliminate([augmented(total, rr)], r)
     alpha_t = six_lanes(alpha.T)
     sol_ref[...] = solution + mxu(alpha_t, six_rows(dst[me], r), NN)
     res_ref[...] = rbuf[me] - mxu(alpha_t, six_rows(q_stacked, r), NN)
@@ -340,7 +347,7 @@
         scratch_shapes=[
             pltpu.VMEM((n, f + r, width), F32),
             pltpu.VMEM((ITERS - 1, n, r, width), F32),
-            pltpu.VMEM((n, r, 128), F32),
+            pltpu.VMEM((n, r * r // 128, 128), F32),
             pltpu.VMEM((n, width, width), BF16),
             pltpu.VMEM((n, width, width), BF16),
             pltpu.VMEM((n, 3 * r, width), BF16),
@@ -348,7 +355,6 @@
             pltpu.VMEM((n, r, width), F32),
             pltpu.VMEM((width, 6 * f), BF16),
             pltpu.VMEM((width, width), F32),
-            pltpu.VMEM((r, width), F32),
             pltpu.VMEM((r, width), F32),
             pltpu.VMEM((3 * r, width), F32),
             pltpu.VMEM((2 * r, width), F32),
@@ -363,7 +369,7 @@
         compiler_params=pltpu.CompilerParams(
             collective_id=0, has_side_effects=True, vmem_limit_bytes=56 * 1024 * 1024
         ),
-    )(points, lengthscales[:, None], noise[None, :], targets)
+    )(points, lengthscales[None, :], noise[None, :], targets)
 
 
 def solution(mesh):

time: 65.7 us -> 60.2 us (0.916); the launches traced: 64.6 us -> 60 us
  Pallas kernels: 60.6 us -> 57.3 us
  local copies, waits for them, and re-layouts: 3.34 us -> 2 us
    pallas_call x1, Pallas kernels: 60.6 us -> 57.3 us  [body(): pl.pallas_call(functools.partial(kernel, n, wide), out_shape=(block, bloc...]
    broadcast_in_dim x1 -> x0, local copies, waits for them, and re-layouts: 0.69 us -> none  [body(): lengthscales[:, None]]
    unnamed x6 -> x4, local copies, waits for them, and re-layouts: 2.65 us -> 2 us
where the time goes in v3:
time: 60.2 us; the launch traced here: 60 us
  Pallas kernels  57.3 us (95%)
  local copies, waits for them, and re-layouts  2 us (3%)
  between operations  0.65 us (1%)
    pallas_call x1, Pallas kernels, body(): pl.pallas_call(functools.partial(kernel, n, wide), out_shape=(block, bloc...  57.3 us
    unnamed x4, local copies, waits for them, and re-layouts  2 us

profile of v3, /device:TPU:0, one launch (start us, length us, event | category | flops | bytes accessed | tf_op | source)
XLA Modules:
  0.0 60.0 jit_solution(18204482326804222149)
XLA Ops:
  0.6 57.3 %shard_map.59 = (f32[32,256]{1,0:T(8,128)}, f32[32,256]{1,0:T(8,128)}) custom-call(f32[32,256]{1,0:T(8,128)} %pts_ref.1, f32[1,32]{1,0:T(1,128)} %bitcast.3, f32[1,256]{1,0:T(1,128)} %bitcast.2, f32[32,256]{1,0:T(8,128)} %tgt_ref.1), custom_call_target="tpu_custom_call" | custom-call | tf_op jit(solution)/shard_map/pallas_call | solution.py:342
  58.0 0.0 copy-start
  58.0 1.4 %copy.8 = f32[32,256]{1,0:T(8,128)} copy(f32[32,256]{1,0:T(8,128)} %get-tuple-element.4) | data formatting | bytes 65536
  59.4 0.0 copy-done
  59.4 0.6 %copy.9 = f32[32,256]{1,0:T(8,128)} copy(f32[32,256]{1,0:T(8,128)S(1)} %copy-done) | data formatting | bytes 65536
Async XLA Ops:
  58.0 1.4 %copy-start = (f32[32,256]{1,0:T(8,128)S(1)}, f32[32,256]{1,0:T(8,128)}, u32[]{:S(2)}) copy-start(f32[32,256]{1,0:T(8,128)} %get-tuple-element.5) | copy-start | bytes 98308

commit v4 on v3

--- a/solution.py
+++ b/solution.py
@@ -87,7 +87,7 @@
 
 def kernel(
     n, wide, pts_ref, ls_ref, noise_ref, tgt_ref, sol_ref, res_ref,
-    gbuf, qbuf, pbuf, kth, ktl, dst, qst, rbuf, own_t, own_n, q_own,
+    gbuf, qbuf, pbuf, kth, ktl, dst, qst, rbuf, own_t, own_n, q_own, q_old,
     acc_h, acc_l, gram,
     send_z, send_y, send_k, recv, send_p, recv_p,
 ):
@@ -152,8 +152,13 @@
             along_y(rnd, buf, 0, dy).start()
         across(rnd, buf, 0, 0).start()
 
-    def gather_use(rnd, buf, use, batch):
-        use([me])
+    def gather_use(rnd, buf, use, batch, after_first=None):
+        late = after_first is not None
+        if not late:
+            use([me])
+
+        def use_line(dy):
+            loop(0, deep // batch, lambda s: use([device(deep - s * batch - i, wide - dy) for i in range(batch)]))
 
         def lane(dz):
             copy = across(rnd, buf, dz, 0)
@@ -161,18 +166,25 @@
             for dy in range(1, wide):
                 along_y(rnd, buf, dz, dy).start()
             copy.start()
-            use([device(deep - dz, 0)])
+            if not late:
+                use([device(deep - dz, 0)])
 
         loop(1, deep, lane)
+        if late:
+            after_first()
+            use_line(0)
         for dy in range(1, wide):
 
             def plane(dz, dy=dy):
                 copy = across(rnd, buf, dz, dy)
                 copy.wait_recv()
                 copy.start()
-                use([device(deep - dz, wide - dy)])
+                if not late:
+                    use([device(deep - dz, wide - dy)])
 
             loop(0, deep, plane)
+            if late:
+                use_line(dy)
 
         def other(s):
             slots = []
@@ -223,44 +235,55 @@
 
     solution = jnp.zeros((r, width), F32)
     image_r = operator(tgt_ref[...])
-    q_own[...] = image_r
+    qbuf[0, me] = image_r
+    gather_start(1, qbuf.at[0])
     for step in range(ITERS - 1):
         buf = qbuf.at[step]
-        buf[me] = q_own[...]
-        gather_start(step + 1, buf)
-        if step > 0:
-
-            def directions(s, beta_t=beta_t):
-                slots = [s * 4 + i for i in range(4)]
-                value = lanes([rbuf[slot] for slot in slots]) + mxu(
-                    beta_t, six_rows(lanes([dst[slot] for slot in slots]), r), NN
-                )
-                stacked = stack3(value)
-                for i, slot in enumerate(slots):
-                    dst[slot] = stacked[:, i * width : (i + 1) * width]
-
-            loop(0, n // 4, directions)
+        beta_t = None if step == 0 else beta_t
+
+        def directions(s, beta_t=beta_t):
+            slots = [s * 4 + i for i in range(4)]
+            value = lanes([rbuf[slot] for slot in slots]) + mxu(
+                beta_t, six_rows(lanes([dst[slot] for slot in slots]), r), NN
+            )
+            stacked = stack3(value)
+            for i, slot in enumerate(slots):
+                dst[slot] = stacked[:, i * width : (i + 1) * width]
+
+        def advance(step=step, directions=directions):
+            if step > 0:
+                loop(0, n // 4, directions)
+
         gram[...] = jnp.zeros_like(gram)
         acc_h[...] = jnp.zeros_like(acc_h)
         acc_l[...] = jnp.zeros_like(acc_l)
 
-        def curvature(slots, buf=buf):
-            stacks = [stack3(buf[slot]) for slot in slots]
-            stacked = lanes(stacks)
+        def curvature(slots, buf=buf, beta_t=beta_t):
+            value = lanes([buf[slot] for slot in slots])
+            if beta_t is not None:
+                value = value + mxu(beta_t, six_rows(lanes([qst[slot] for slot in slots]), r), NN)
+            stacked = stack3(value)
             gram[...] += mxu(lanes([dst[slot] for slot in slots]), stacked, NT)
             acc_h[...] += mxu(stacked, lanes([kth[slot] for slot in slots]), NT)
             acc_l[...] += mxu(stacked[: 2 * r], lanes([ktl[slot] for slot in slots]), NT)
-            for slot, stack in zip(slots, stacks):
-                qst[slot] = stack
-
-        gather_use(step + 1, buf, curvature, 4)
+            for i, slot in enumerate(slots):
+                qst[slot] = stacked[:, i * width : (i + 1) * width]
+
+        gather_use(step + 1, buf, curvature, 4, advance)
         alpha, rr_inv = eliminate(
             [augmented(fold_gram(gram[...], r), rr), augmented(rr, eye)], r
         )
         alpha_t = six_lanes(alpha.T)
         solution = solution + mxu(alpha_t, six_rows(dst[me], r), NN)
-        image_q = operator(q_own[...])
+        image = image_r
+        if step > 0:
+            image = image_r + mxu(beta_t, six_rows(q_old[...], r), NN)
+        image_q = operator(image)
         image_r = image_r - mxu(alpha_t, six_rows(stack3(image_q), r), NN)
+        if step + 2 < ITERS:
+            qbuf[step + 1, me] = image_r
+            gather_start(step + 2, qbuf.at[step + 1])
+            q_old[...] = qst[me]
         gram[...] = jnp.zeros_like(gram)
 
         def residuals(s, alpha_t=alpha_t):
@@ -356,6 +379,7 @@
             pltpu.VMEM((width, 6 * f), BF16),
             pltpu.VMEM((width, width), F32),
             pltpu.VMEM((r, width), F32),
+            pltpu.VMEM((3 * r, width), BF16),
             pltpu.VMEM((3 * r, width), F32),
             pltpu.VMEM((2 * r, width), F32),
             pltpu.VMEM((3 * r, 3 * r), F32),

time: 60.2 us -> 58.9 us (0.978)
  Pallas kernels: 57.3 us -> 56 us
    pallas_call x1, Pallas kernels: 57.3 us -> 56 us  [body(): pl.pallas_call(functools.partial(kernel, n, wide), out_shape=(block, bloc...]
where the time goes in v4:
time: 58.9 us; the launch traced here: 58.7 us
  Pallas kernels  56 us (95%)
  local copies, waits for them, and re-layouts  2 us (3%)
  between operations  0.65 us (1%)
    pallas_call x1, Pallas kernels, body(): pl.pallas_call(functools.partial(kernel, n, wide), out_shape=(block, bloc...  56 us
    unnamed x4, local copies, waits for them, and re-layouts  2 us

profile of v4, /device:TPU:0, one launch (start us, length us, event | category | flops | bytes accessed | tf_op | source)
XLA Modules:
  0.0 58.7 jit_solution(10364306989810141729)
XLA Ops:
  0.6 56.0 %shard_map.59 = (f32[32,256]{1,0:T(8,128)}, f32[32,256]{1,0:T(8,128)}) custom-call(f32[32,256]{1,0:T(8,128)} %pts_ref.1, f32[1,32]{1,0:T(1,128)} %bitcast.3, f32[1,256]{1,0:T(1,128)} %bitcast.2, f32[32,256]{1,0:T(8,128)} %tgt_ref.1), custom_call_target="tpu_custom_call" | custom-call | tf_op jit(solution)/shard_map/pallas_call | solution.py:365
  56.7 0.0 copy-start
  56.7 1.4 %copy.8 = f32[32,256]{1,0:T(8,128)} copy(f32[32,256]{1,0:T(8,128)} %get-tuple-element.4) | data formatting | bytes 65536
  58.1 0.0 copy-done
  58.1 0.6 %copy.9 = f32[32,256]{1,0:T(8,128)} copy(f32[32,256]{1,0:T(8,128)S(1)} %copy-done) | data formatting | bytes 65536
Async XLA Ops:
  56.7 1.4 %copy-start = (f32[32,256]{1,0:T(8,128)S(1)}, f32[32,256]{1,0:T(8,128)}, u32[]{:S(2)}) copy-start(f32[32,256]{1,0:T(8,128)} %get-tuple-element.5) | copy-start | bytes 98308

commit v5 on v4

--- a/solution.py
+++ b/solution.py
@@ -86,7 +86,7 @@
 
 
 def kernel(
-    n, wide, pts_ref, ls_ref, noise_ref, tgt_ref, sol_ref, res_ref,
+    n, wide, pts_ref, ls_ref, noise_ref, tgt_ref, out_ref,
     gbuf, qbuf, pbuf, kth, ktl, dst, qst, rbuf, own_t, own_n, q_own, q_old,
     acc_h, acc_l, gram,
     send_z, send_y, send_k, recv, send_p, recv_p,
@@ -332,8 +332,8 @@
     total = jnp.concatenate([total[:, i : i + r] for i in range(0, 128, r)], axis=0)
     (alpha,) = eliminate([augmented(total, rr)], r)
     alpha_t = six_lanes(alpha.T)
-    sol_ref[...] = solution + mxu(alpha_t, six_rows(dst[me], r), NN)
-    res_ref[...] = rbuf[me] - mxu(alpha_t, six_rows(q_stacked, r), NN)
+    out_ref[:r, :] = solution + mxu(alpha_t, six_rows(dst[me], r), NN)
+    out_ref[r:, :] = rbuf[me] - mxu(alpha_t, six_rows(q_stacked, r), NN)
 
     for rnd in range(ITERS):
         buf = gbuf if rnd == 0 else qbuf.at[rnd - 1]
@@ -357,16 +357,16 @@
 def body(n, points, lengthscales, noise, targets):
     f, width = points.shape
     r = targets.shape[0]
-    block = jax.ShapeDtypeStruct((r, width), F32)
+    block = jax.ShapeDtypeStruct((2 * r, width), F32)
     chips = n // 2
     wide = 2 if chips % 2 == 0 and chips <= 8 else 1
     deep = chips // wide
     vmem = pl.BlockSpec(memory_space=pltpu.VMEM)
-    return pl.pallas_call(
+    out = pl.pallas_call(
         functools.partial(kernel, n, wide),
-        out_shape=(block, block),
+        out_shape=block,
         in_specs=[vmem] * 4,
-        out_specs=(vmem, vmem),
+        out_specs=vmem,
         scratch_shapes=[
             pltpu.VMEM((n, f + r, width), F32),
             pltpu.VMEM((ITERS - 1, n, r, width), F32),
@@ -394,6 +394,7 @@
             collective_id=0, has_side_effects=True, vmem_limit_bytes=56 * 1024 * 1024
         ),
     )(points, lengthscales[None, :], noise[None, :], targets)
+    return out[:r], out[r:]
 
 
 def solution(mesh):

time: 58.9 us -> 58.4 us (level)
  local copies, waits for them, and re-layouts: 2 us -> 1.4 us
    unnamed x4 -> x0, local copies, waits for them, and re-layouts: 2 us -> none
    slice x0 -> x1, local copies, waits for them, and re-layouts: none -> 1.4 us  [body(): return (out[:r], out[r:])]
where the time goes in v5:
time: 58.4 us; the launch traced here: 58.1 us
  Pallas kernels  56 us (96%)
  local copies, waits for them, and re-layouts  1.4 us (2%)
  between operations  0.64 us (1%)
    pallas_call x1, Pallas kernels, body(): pl.pallas_call(functools.partial(kernel, n, wide), out_shape=block, in_sp...  56 us
    slice x1, local copies, waits for them, and re-layouts, body(): return (out[:r], out[r:])  1.4 us

profile of v5, /device:TPU:0, one launch (start us, length us, event | category | flops | bytes accessed | tf_op | source)
XLA Modules:
  0.0 58.1 jit_solution(895827790599821352)
XLA Ops:
  0.6 56.0 %shard_map.59 = f32[64,256]{1,0:T(8,128)} custom-call(f32[32,256]{1,0:T(8,128)} %pts_ref.1, f32[1,32]{1,0:T(1,128)} %bitcast.3, f32[1,256]{1,0:T(1,128)} %bitcast.2, f32[32,256]{1,0:T(8,128)} %tgt_ref.1), custom_call_target="tpu_custom_call" | custom-call | tf_op jit(solution)/shard_map/pallas_call | solution.py:365
  56.7 1.4 %fusion = (f32[32,256]{1,0:T(8,128)}, f32[32,256]{1,0:T(8,128)}) fusion(f32[64,256]{1,0:T(8,128)} %shard_map.59), kind=kLoop, calls=%fused_computation | loop fusion | bytes 131072 | tf_op jit(solution)/shard_map/slice | solution.py:397

commit v6 on v5

--- a/solution.py
+++ b/solution.py
@@ -242,7 +242,7 @@
         beta_t = None if step == 0 else beta_t
 
         def directions(s, beta_t=beta_t):
-            slots = [s * 4 + i for i in range(4)]
+            slots = [s * 8 + i for i in range(8)]
             value = lanes([rbuf[slot] for slot in slots]) + mxu(
                 beta_t, six_rows(lanes([dst[slot] for slot in slots]), r), NN
             )
@@ -252,7 +252,7 @@
 
         def advance(step=step, directions=directions):
             if step > 0:
-                loop(0, n // 4, directions)
+                loop(0, n // 8, directions)
 
         gram[...] = jnp.zeros_like(gram)
         acc_h[...] = jnp.zeros_like(acc_h)
@@ -287,7 +287,7 @@
         gram[...] = jnp.zeros_like(gram)
 
         def residuals(s, alpha_t=alpha_t):
-            slots = [s * 4 + i for i in range(4)]
+            slots = [s * 8 + i for i in range(8)]
             value = lanes([rbuf[slot] for slot in slots]) - mxu(
                 alpha_t, six_rows(lanes([qst[slot] for slot in slots]), r), NN
             )
@@ -296,7 +296,7 @@
             for i, slot in enumerate(slots):
                 rbuf[slot] = value[:, i * width : (i + 1) * width]
 
-        loop(0, n // 4, residuals)
+        loop(0, n // 8, residuals)
         rr_next = fold_gram(gram[...], r)
         beta = jnp.dot(rr_inv, rr_next, precision=lax.Precision.HIGHEST, preferred_element_type=F32)
         beta_t = six_lanes(beta.T)

time: 58.4 us -> 57.8 us (0.990)
    pallas_call x1, Pallas kernels: 56 us -> 55.5 us  [body(): pl.pallas_call(functools.partial(kernel, n, wide), out_shape=block, in_sp...]
where the time goes in v6:
time: 57.8 us; the launch traced here: 57.5 us
  Pallas kernels  55.5 us (96%)
  local copies, waits for them, and re-layouts  1.4 us (2%)
  between operations  0.64 us (1%)
    pallas_call x1, Pallas kernels, body(): pl.pallas_call(functools.partial(kernel, n, wide), out_shape=block, in_sp...  55.5 us
    slice x1, local copies, waits for them, and re-layouts, body(): return (out[:r], out[r:])  1.4 us

profile of v6, /device:TPU:0, one launch (start us, length us, event | category | flops | bytes accessed | tf_op | source)
XLA Modules:
  0.0 57.5 jit_solution(14196091685798508701)
XLA Ops:
  0.6 55.5 %shard_map.59 = f32[64,256]{1,0:T(8,128)} custom-call(f32[32,256]{1,0:T(8,128)} %pts_ref.1, f32[1,32]{1,0:T(1,128)} %bitcast.3, f32[1,256]{1,0:T(1,128)} %bitcast.2, f32[32,256]{1,0:T(8,128)} %tgt_ref.1), custom_call_target="tpu_custom_call" | custom-call | tf_op jit(solution)/shard_map/pallas_call | solution.py:365
  56.1 1.4 %fusion = (f32[32,256]{1,0:T(8,128)}, f32[32,256]{1,0:T(8,128)}) fusion(f32[64,256]{1,0:T(8,128)} %shard_map.59), kind=kLoop, calls=%fused_computation | loop fusion | bytes 131072 | tf_op jit(solution)/shard_map/slice | solution.py:397
